TPU v7x, 512 devices: a whole 4x8x8 slice. The times are simulated.
512 devices in a mesh: row: 16 (over z, core), col: 32 (over x, y).
Axes of the slice: x: 4, y: 8, z: 8, core: 2. Of those that a mesh axis runs over, the one named last changes fastest.
Arguments:
- state_fields: bfloat16 [4, 16, 16, 16, 32, 256], P(None, None, None, 'row', 'col'), may hold values from -6 to 6
- leaf_solve: float32 [256, 256], replicated, may hold values from -0.375 to 0.375
- leaf_flux: float32 [64, 256], replicated, may hold values from -0.375 to 0.375
- lift_edges: float32 [64, 128], replicated, may hold values from -4 to 4
- lift_leaves: float32 [256, 128], replicated, may hold values from -0.046875 to 0.046875
- merge_interface: float32 [5, 128, 128], replicated, may hold values from -0.25 to 0.25
- merge_parent: float32 [5, 256, 128], replicated, may hold values from -0.375 to 0.375
- split_child: float32 [5, 128, 256], replicated, may hold values from -0.5 to 0.5
- top_inverse: float32 [2048, 2048], P(None, 'row'), may hold values from -0.125 to 0.125
- spread_edges: float32 [64, 128], replicated, may hold values from -4 to 4
- spread_leaves: float32 [256, 128], replicated, may hold values from -0.5 to 0.5
- leaf_extend: float32 [256, 64], replicated, may hold values from -0.375 to 0.375
Outputs:
- new_fields: bfloat16 [4, 16, 16, 16, 32, 256], P(None, None, None, 'row', 'col')
All inputs are finite; a program needn't handle non-finite values.
Results may differ from a plain program's by a relative error of at most 0.0035.
Values may be sent and summed in bfloat16 or wider, within the bound.
A program may use at most 64 MiB of HBM per device.

v0:
```python
import jax
import jax.numpy as jnp
import numpy as np
from jax import lax
from jax.sharding import PartitionSpec as P

SKEL = 128
LR = 4
LC = 64
advect_scale = 0.01
full_precision = lax.Precision.HIGHEST


def extended(x, sides, width):
    for axis, dim in sides:
        devices, length = (lax.axis_size(axis), x.shape[dim])
        up = [(i, (i + 1) % devices) for i in range(devices)]
        down = [(j, i) for i, j in up]
        last = lax.slice_in_dim(x, length - width, length, axis=dim)
        first = lax.slice_in_dim(x, 0, width, axis=dim)
        before = lax.ppermute(last, axis, up)
        after = lax.ppermute(first, axis, down)
        x = jnp.concatenate([before, x, after], axis=dim)
    return x


def partner_2(block, axis, stride):
    count = lax.axis_size(axis)
    route = []
    for low in range(count):
        high = low | 1 << stride
        if high != low and high < count:
            route += [(low, high), (high, low)]
    return lax.ppermute(block, axis, route)


def chebyshev_matrix(node_count):
    points = np.arange(node_count)
    grid_x = np.cos(np.pi * points / (node_count - 1))
    weights = np.where(points == 0, 2.0, np.where(points == node_count - 1, 2.0, 1.0))
    parity = np.where((points[:, None] + points[None, :]) % 2 == 0, 1.0, -1.0)
    identity = np.eye(node_count)
    spacing = grid_x[:, None] - grid_x[None, :] + identity
    off_diagonal = weights[:, None] / weights[None, :] * parity / spacing * (1.0 - identity)
    result_matrix = off_diagonal - identity * off_diagonal.sum(axis=1)[:, None]
    return jnp.asarray(result_matrix, dtype=jnp.float32)


def tendency(values):
    derivative = chebyshev_matrix(values.shape[1])
    along_rows = jnp.einsum("ik,fkjrc->fijrc", derivative, values, precision=full_precision)
    along_cols = jnp.einsum("jk,fikrc->fijrc", derivative, values, precision=full_precision)
    return advect_scale * (values[0:1] * along_rows + values[1:2] * along_cols)


def average_rows(values, north_in, south_in):
    above = jnp.concatenate([north_in, values[:, -1, :, :-1, :]], axis=2)
    below = jnp.concatenate([values[:, 0, :, 1:, :], south_in], axis=2)
    first_row = (values[:, 0] + above) * 0.5
    last_row = (values[:, -1] + below) * 0.5
    return jnp.concatenate([first_row[:, None], values[:, 1:-1], last_row[:, None]], axis=1)


def average_cols(values, west_in, east_in):
    left_side = jnp.concatenate([west_in, values[:, :, -1, :, :-1]], axis=3)
    right_side = jnp.concatenate([values[:, :, 0, :, 1:], east_in], axis=3)
    first_col = (values[:, :, 0] + left_side) * 0.5
    last_col = (values[:, :, -1] + right_side) * 0.5
    return jnp.concatenate(
        [first_col[:, :, None], values[:, :, 1:-1], last_col[:, :, None]], axis=2
    )


def local(
    state_fields,
    leaf_solve,
    leaf_flux,
    lift_edges,
    lift_leaves,
    merge_interface,
    merge_parent,
    split_child,
    top_inverse,
    spread_edges,
    spread_leaves,
    leaf_extend,
):
    field_count = state_fields.shape[0]
    node_count = state_fields.shape[1]
    leaf_total = state_fields.shape[-1]
    local_grid = state_fields.reshape(field_count, node_count, node_count, LR, LC)
    widened = extended(local_grid, (("row", 3), ("col", 4)), 1)
    pushed = tendency(widened.astype(jnp.float32))
    rows_done = average_rows(pushed, pushed[:, -1][:, :, :1, :], pushed[:, 0][:, :, -1:, :])
    both_done = average_cols(
        rows_done, rows_done[:, :, -1][:, :, :, :1], rows_done[:, :, 0][:, :, :, -1:]
    )
    averaged = both_done[:, :, :, 1:-1, 1:-1]
    values = local_grid.astype(jnp.float32)
    source = (values - averaged).reshape(field_count, node_count * node_count, leaf_total)
    particular = jnp.einsum("nm,fml->fnl", leaf_solve, source, precision=full_precision)
    edge_flux = jnp.einsum("em,fml->fel", leaf_flux, source, precision=full_precision)
    lifted = jnp.einsum("fel,lb->feb", edge_flux, lift_leaves, precision=full_precision)
    skeleton = jnp.sum(lifted * lift_edges[None], axis=1)
    column = lax.axis_index("col")
    level_count = lax.axis_size("col").bit_length() - 1
    interfaces = []
    for merge_level in range(level_count):
        stride = 1 << merge_level
        partner = partner_2(skeleton, "col", merge_level)
        on_left = column // stride % 2 == 0
        left_half = jnp.where(on_left, skeleton, partner)
        right_half = jnp.where(on_left, partner, skeleton)
        interfaces.append(
            jnp.dot(right_half - left_half, merge_interface[merge_level], precision=full_precision)
        )
        joined = jnp.concatenate([left_half, right_half], axis=-1)
        skeleton = jnp.dot(joined, merge_parent[merge_level], precision=full_precision)
    shard_piece = lax.all_gather(skeleton[None], "row", axis=0, tiled=True)
    piece_rows = shard_piece.shape[0]
    top_rows = top_inverse
    top_rows = top_rows.reshape(piece_rows, SKEL, SKEL)
    boundary = jnp.einsum("gfb,gbc->fc", shard_piece, top_rows, precision=full_precision)
    for merge_level in reversed(range(level_count)):
        stride = 1 << merge_level
        child_map = split_child[merge_level]
        left_half = (
            jnp.dot(boundary, child_map[:, :SKEL], precision=full_precision)
            + interfaces[merge_level]
        )
        right_half = (
            jnp.dot(boundary, child_map[:, SKEL:], precision=full_precision)
            + interfaces[merge_level]
        )
        boundary = jnp.where(column // stride % 2 == 0, left_half, right_half)
    weighted = boundary[:, None, :] * spread_edges[None]
    spread = jnp.einsum("feb,lb->fel", weighted, spread_leaves, precision=full_precision)
    solved = particular + jnp.einsum("ne,fel->fnl", leaf_extend, spread, precision=full_precision)
    return solved.reshape(field_count, node_count, node_count, 1, 1, leaf_total).astype(
        jnp.bfloat16
    )


def solution(mesh):
    in_specs = (
        P(None, None, None, "row", "col", None),
        P(),
        P(),
        P(),
        P(),
        P(),
        P(),
        P(),
        P(None, "row"),
        P(),
        P(),
        P(),
    )
    out_specs = P(None, None, None, "row", "col", None)
    return jax.shard_map(local, mesh=mesh, in_specs=in_specs, out_specs=out_specs, check_vma=False)
```

profile of v0, /device:TPU:1, one launch (start us, length us, event | category | flops | bytes accessed | tf_op | source)
XLA Modules:
  0.0 127.9 jit_solution(2190358243321352747)
XLA Ops:
  0.0 2.1 %reshape.38 = bf16[4,16,16,4,64]{4,3,2,1,0:T(4,128)(2,1)S(1)} reshape(bf16[4,16,16,1,1,256]{5,2,4,3,1,0:T(8,128)(2,1)} %param.13) | data formatting | bytes 1048576 | tf_op jit(solution)/shard_map/reshape | solution.py:91
  3.1 3.5 %collective-permute-start = (bf16[4,16,16,1,64]{4,1,3,2,0:T(8,128)(2,1)S(1)}, bf16[4,16,16,1,64]{4,1,3,2,0:T(8,128)(2,1)S(1)}, u32[]{:S(2)}, u32[]{:S(2)}) collective-permute-start(bf16[4,16,16,1,64]{4,1,3,2,0:T(8,128)(2,1)S(1)} %copy.84), channel_id=1, source_target_pairs={{0,32},{32,64},{64,96},{96,128},{128,160},{160,192},{192,224},{224... | collective-permute-start | bytes 393224 | tf_op jit(solution)/shard_map/ppermute | solution.py:21
  6.7 3.4 %collective-permute-start.1 = (bf16[4,16,16,1,64]{4,1,3,2,0:T(8,128)(2,1)S(1)}, bf16[4,16,16,1,64]{4,1,3,2,0:T(8,128)(2,1)S(1)}, u32[]{:S(2)}, u32[]{:S(2)}) collective-permute-start(bf16[4,16,16,1,64]{4,1,3,2,0:T(8,128)(2,1)S(1)} %copy.85), channel_id=1, source_target_pairs={{32,0},{64,32},{96,64},{128,96},{160,128},{192,160},{224,192},{256... | collective-permute-start | bytes 393224 | tf_op jit(solution)/shard_map/ppermute | solution.py:22
  12.6 2.4 %fusion.99 = (bf16[4,16,16,6,1]{4,1,3,2,0:T(8,128)(2,1)}, bf16[4,16,16,6,1]{4,1,3,2,0:T(8,128)(2,1)}) fusion(bf16[4,16,16,6,64]{4,1,3,2,0:T(8,128)(2,1)S(1)} %constant_dynamic-update-slice_fusion), kind=kLoop, calls=%fused_computation.150 | loop fusion | bytes 49152 | tf_op jit(solution)/shard_map/slice | solution.py:19
  14.9 3.7 %copy.58 = bf16[4,16,16,6,1]{2,1,4,3,0:T(8,128)(2,1)S(1)} copy(bf16[4,16,16,6,1]{4,1,3,2,0:T(8,128)(2,1)} %get-tuple-element.19) | data formatting | bytes 24576 | tf_op jit(solution)/shard_map/slice | solution.py:19
  18.6 3.2 %collective-permute-start.2 = (bf16[4,16,16,6,1]{2,1,4,3,0:T(8,128)(2,1)S(1)}, bf16[4,16,16,6,1]{2,1,4,3,0:T(8,128)(2,1)}, u32[]{:S(2)}, u32[]{:S(2)}) collective-permute-start(bf16[4,16,16,6,1]{2,1,4,3,0:T(8,128)(2,1)S(1)} %copy.58), channel_id=1, source_target_pairs={{0,1},{1,2},{2,3},{3,4},{4,5},{5,6},{6,7},{7,8},{8,9},{9,10},{10,1... | collective-permute-start | bytes 36872 | tf_op jit(solution)/shard_map/ppermute | solution.py:21
  21.8 4.2 %copy.59 = bf16[4,16,16,6,1]{2,1,4,3,0:T(8,128)(2,1)} copy(bf16[4,16,16,6,1]{4,1,3,2,0:T(8,128)(2,1)} %get-tuple-element.20) | data formatting | bytes 24576 | tf_op jit(solution)/shard_map/slice | solution.py:20
  26.0 6.0 %collective-permute-start.3 = (bf16[4,16,16,6,1]{2,1,4,3,0:T(8,128)(2,1)}, bf16[4,16,16,6,1]{2,1,4,3,0:T(8,128)(2,1)}, u32[]{:S(2)}, u32[]{:S(2)}) collective-permute-start(bf16[4,16,16,6,1]{2,1,4,3,0:T(8,128)(2,1)} %copy.59), channel_id=1, source_target_pairs={{1,0},{2,1},{3,2},{4,3},{5,4},{6,5},{7,6},{8,7},{9,8},{10,9},{11,1... | collective-permute-start | bytes 36872 | tf_op jit(solution)/shard_map/ppermute | solution.py:22
  32.2 4.6 %copy.60 = bf16[4,16,16,6,1]{4,1,3,2,0:T(8,128)(2,1)} copy(bf16[4,16,16,6,1]{2,1,4,3,0:T(8,128)(2,1)} %collective-permute-done.2) | data formatting | bytes 24576 | tf_op jit(solution)/shard_map/ppermute | solution.py:21
  36.8 4.6 %copy.61 = bf16[4,16,16,6,1]{4,1,3,2,0:T(8,128)(2,1)} copy(bf16[4,16,16,6,1]{2,1,4,3,0:T(8,128)(2,1)} %collective-permute-done.3) | data formatting | bytes 24576 | tf_op jit(solution)/shard_map/ppermute | solution.py:22
  41.4 3.8 %fusion.96 = (f32[4,16,16,6,66]{4,1,3,2,0:T(8,128)S(1)}, bf16[4,16,16,6,66]{4,1,3,2,0:T(8,128)(2,1)S(1)}) fusion(bf16[4,16,16,6,1]{4,1,3,2,0:T(8,128)(2,1)} %copy.61, bf16[4,16,16,6,64]{4,1,3,2,0:T(8,128)(2,1)} %copy-done.2, bf16[4,16,16,6,1]{4,1,3,2,0:T(8,128)(2,1)} %copy.60), kind=kLoop, calls=%fused_computation.147 | loop fusion | flops 2838528 | bytes 3244032 | tf_op jit(solution)/shard_map/convert_element_type | solution.py:93
  47.4 3.5 %fusion.1 = f32[4,16,16,6,66]{4,1,3,2,0:T(8,128)S(1)} fusion(f32[4,16,6,66,16]{3,4,2,1,0:T(8,128)S(1)} %fusion.3, bf16[4,16,16,6,66]{4,1,3,2,0:T(8,128)(2,1)S(1)} %get-tuple-element.6, f32[16,16,1,1,1]{1,0,4,3,2:T(8,128)S(1)} %copy-done.14, f32[16,16,6,66]{3,0,2,1:T(8,128)S(1)} %get-tuple-element.18, f32[16,16,6,66]{3,0,2,1:T(8,128)S(1)} %get-tuple-element.17), kind=kOutput, calls=%fused_computation.3 | convolution fusion | flops 79478784 | bytes 4867072 | tf_op jit(solution)/shard_map/ik,fkjrc->fijrc/dot_general | solution.py:51
  59.7 2.4 %copy.72 = f32[4,16,16,4,64]{4,3,2,1,0:T(4,128)} copy(f32[4,16,16,4,64]{4,1,3,2,0:T(8,128)S(1)} %fusion.2) | data formatting | bytes 2097152 | tf_op jit(solution)/shard_map/sub | solution.py:100
  62.1 2.5 %reshape.39 = f32[4,256,256]{2,1,0:T(8,128)S(1)} reshape(f32[4,16,16,4,64]{4,3,2,1,0:T(4,128)} %copy.72) | data formatting | bytes 2097152 | tf_op jit(solution)/shard_map/reshape | solution.py:100
  65.9 2.1 %collective-permute-start.4 = (f32[4,128]{1,0:T(4,128)S(1)}, f32[4,128]{1,0:T(4,128)S(1)}, u32[]{:S(2)}, u32[]{:S(2)}) collective-permute-start(f32[4,128]{1,0:T(4,128)S(1)} %fusion.6), channel_id=1, source_target_pairs={{0,1},{1,0},{2,3},{3,2},{4,5},{5,4},{6,7},{7,6},{8,9},{9,8},{10,11... | collective-permute-start | bytes 6152 | tf_op jit(solution)/shard_map/ppermute | solution.py:34
  70.6 1.9 %collective-permute-start.5 = (f32[4,128]{1,0:T(4,128)S(1)}, f32[4,128]{1,0:T(4,128)S(1)}, u32[]{:S(2)}, u32[]{:S(2)}) collective-permute-start(f32[4,128]{1,0:T(4,128)S(1)} %fusion.33), channel_id=1, source_target_pairs={{0,2},{2,0},{1,3},{3,1},{4,6},{6,4},{5,7},{7,5},{8,10},{10,8},{9,1... | collective-permute-start | bytes 6152 | tf_op jit(solution)/shard_map/ppermute | solution.py:34
  72.7 3.1 %collective-permute-done.5 = f32[4,128]{1,0:T(4,128)S(1)} collective-permute-done((f32[4,128]{1,0:T(4,128)S(1)}, f32[4,128]{1,0:T(4,128)S(1)}, u32[]{:S(2)}, u32[]{:S(2)}) %collective-permute-start.5) | collective-permute-done | bytes 2080 | tf_op jit(solution)/shard_map/ppermute | solution.py:34
  76.0 4.7 %collective-permute-start.6 = (f32[4,128]{1,0:T(4,128)S(1)}, f32[4,128]{1,0:T(4,128)S(1)}, u32[]{:S(2)}, u32[]{:S(2)}) collective-permute-start(f32[4,128]{1,0:T(4,128)S(1)} %fusion.31), channel_id=1, source_target_pairs={{0,4},{4,0},{1,5},{5,1},{2,6},{6,2},{3,7},{7,3},{8,12},{12,8},{9,1... | collective-permute-start | bytes 6152 | tf_op jit(solution)/shard_map/ppermute | solution.py:34
  80.9 3.3 %collective-permute-done.6 = f32[4,128]{1,0:T(4,128)S(1)} collective-permute-done((f32[4,128]{1,0:T(4,128)S(1)}, f32[4,128]{1,0:T(4,128)S(1)}, u32[]{:S(2)}, u32[]{:S(2)}) %collective-permute-start.6) | collective-permute-done | bytes 2080 | tf_op jit(solution)/shard_map/ppermute | solution.py:34
  84.4 1.9 %collective-permute-start.7 = (f32[4,128]{1,0:T(4,128)S(1)}, f32[4,128]{1,0:T(4,128)S(1)}, u32[]{:S(2)}, u32[]{:S(2)}) collective-permute-start(f32[4,128]{1,0:T(4,128)S(1)} %fusion.29), channel_id=1, source_target_pairs={{0,8},{8,0},{1,9},{9,1},{2,10},{10,2},{3,11},{11,3},{4,12},{12,4},... | collective-permute-start | bytes 6152 | tf_op jit(solution)/shard_map/ppermute | solution.py:34
  86.5 2.2 %collective-permute-done.7 = f32[4,128]{1,0:T(4,128)S(1)} collective-permute-done((f32[4,128]{1,0:T(4,128)S(1)}, f32[4,128]{1,0:T(4,128)S(1)}, u32[]{:S(2)}, u32[]{:S(2)}) %collective-permute-start.7) | collective-permute-done | bytes 2080 | tf_op jit(solution)/shard_map/ppermute | solution.py:34
  88.9 2.8 %collective-permute-start.8 = (f32[4,128]{1,0:T(4,128)S(1)}, f32[4,128]{1,0:T(4,128)S(1)}, u32[]{:S(2)}, u32[]{:S(2)}) collective-permute-start(f32[4,128]{1,0:T(4,128)S(1)} %fusion.27), channel_id=1, source_target_pairs={{0,16},{16,0},{1,17},{17,1},{2,18},{18,2},{3,19},{19,3},{4,20},{20... | collective-permute-start | bytes 6152 | tf_op jit(solution)/shard_map/ppermute | solution.py:34
  91.9 2.8 %collective-permute-done.8 = f32[4,128]{1,0:T(4,128)S(1)} collective-permute-done((f32[4,128]{1,0:T(4,128)S(1)}, f32[4,128]{1,0:T(4,128)S(1)}, u32[]{:S(2)}, u32[]{:S(2)}) %collective-permute-start.8) | collective-permute-done | bytes 2080 | tf_op jit(solution)/shard_map/ppermute | solution.py:34
  95.1 28.3 %all-gather.1 = f32[16,4,128]{2,1,0:T(4,128)S(1)} all-gather(f32[1,4,128]{2,1,0:T(4,128)S(1)} %convolution_bitcast_fusion.2), channel_id=2, replica_groups=mesh['row'=16,'col'=32] {'row'}, dimensions={0}, use_global_device_ids=true | all-gather | bytes 34816 | tf_op jit(solution)/shard_map/all_gather | solution.py:119
  (93 shorter events, 24.3 us)
Async XLA Ops:
  0.0 123.3 %copy-start = (f32[2048,128]{1,0:T(8,128)S(1)}, f32[2048,128]{1,0:T(8,128)}, u32[]{:S(2)}) copy-start(f32[2048,128]{1,0:T(8,128)} %param.21) | copy-start | bytes 3145732
  3.1 7.9 %collective-permute-start = (bf16[4,16,16,1,64]{4,1,3,2,0:T(8,128)(2,1)S(1)}, bf16[4,16,16,1,64]{4,1,3,2,0:T(8,128)(2,1)S(1)}, u32[]{:S(2)}, u32[]{:S(2)}) collective-permute-start(bf16[4,16,16,1,64]{4,1,3,2,0:T(8,128)(2,1)S(1)} %copy.84), channel_id=1, source_target_pairs={{0,32},{32,64},{64,96},{96,128},{128,160},{160,192},{192,224},{224... | collective-permute-start | bytes 393224 | tf_op jit(solution)/shard_map/ppermute | solution.py:21
  6.7 5.8 %collective-permute-start.1 = (bf16[4,16,16,1,64]{4,1,3,2,0:T(8,128)(2,1)S(1)}, bf16[4,16,16,1,64]{4,1,3,2,0:T(8,128)(2,1)S(1)}, u32[]{:S(2)}, u32[]{:S(2)}) collective-permute-start(bf16[4,16,16,1,64]{4,1,3,2,0:T(8,128)(2,1)S(1)} %copy.85), channel_id=1, source_target_pairs={{32,0},{64,32},{96,64},{128,96},{160,128},{192,160},{224,192},{256... | collective-permute-start | bytes 393224 | tf_op jit(solution)/shard_map/ppermute | solution.py:22
  12.6 2.4 %copy-start.2 = (bf16[4,16,16,6,64]{4,1,3,2,0:T(8,128)(2,1)}, bf16[4,16,16,6,64]{4,1,3,2,0:T(8,128)(2,1)S(1)}, u32[]{:S(2)}) copy-start(bf16[4,16,16,6,64]{4,1,3,2,0:T(8,128)(2,1)S(1)} %constant_dynamic-update-slice_fusion) | copy-start | bytes 2359300
  14.9 17.1 %copy-start.4 = (f32[5,128,256]{2,1,0:T(8,128)S(1)}, f32[5,128,256]{2,1,0:T(8,128)}, u32[]{:S(2)}) copy-start(f32[5,128,256]{2,1,0:T(8,128)} %param.20) | copy-start | bytes 1966084
  18.6 13.6 %collective-permute-start.2 = (bf16[4,16,16,6,1]{2,1,4,3,0:T(8,128)(2,1)S(1)}, bf16[4,16,16,6,1]{2,1,4,3,0:T(8,128)(2,1)}, u32[]{:S(2)}, u32[]{:S(2)}) collective-permute-start(bf16[4,16,16,6,1]{2,1,4,3,0:T(8,128)(2,1)S(1)} %copy.58), channel_id=1, source_target_pairs={{0,1},{1,2},{2,3},{3,4},{4,5},{5,6},{6,7},{7,8},{8,9},{9,10},{10,1... | collective-permute-start | bytes 36872 | tf_op jit(solution)/shard_map/ppermute | solution.py:21
  26.0 10.8 %collective-permute-start.3 = (bf16[4,16,16,6,1]{2,1,4,3,0:T(8,128)(2,1)}, bf16[4,16,16,6,1]{2,1,4,3,0:T(8,128)(2,1)}, u32[]{:S(2)}, u32[]{:S(2)}) collective-permute-start(bf16[4,16,16,6,1]{2,1,4,3,0:T(8,128)(2,1)} %copy.59), channel_id=1, source_target_pairs={{1,0},{2,1},{3,2},{4,3},{5,4},{6,5},{7,6},{8,7},{9,8},{10,9},{11,1... | collective-permute-start | bytes 36872 | tf_op jit(solution)/shard_map/ppermute | solution.py:22
  51.8 1.6 %copy-start.1 = (f32[4,14,16,6,66]{4,1,3,2,0:T(8,128)}, f32[4,14,16,6,66]{4,1,3,2,0:T(8,128)S(1)}, u32[]{:S(2)}) copy-start(f32[4,14,16,6,66]{4,1,3,2,0:T(8,128)S(1)} %slice.198) | copy-start | bytes 4257796
  53.4 1.7 %copy-start.3 = (f32[4,16,16,6,66]{4,1,3,2,0:T(8,128)}, f32[4,16,16,6,66]{4,1,3,2,0:T(8,128)S(1)}, u32[]{:S(2)}) copy-start(f32[4,16,16,6,66]{4,1,3,2,0:T(8,128)S(1)} %pad_maximum_fusion) | copy-start | bytes 4866052
  56.1 2.1 %slice-start = ((f32[4,16,16,6,66]{4,1,3,2,0:T(8,128)}), f32[4,16,14,6,66]{4,1,3,2,0:T(8,128)S(1)}, s32[]{:S(2)}) async-start(f32[4,16,16,6,66]{4,1,3,2,0:T(8,128)} %copy-done.3), calls=%async_computation | async-start | bytes 5505024 | tf_op jit(solution)/shard_map/slice | solution.py:70
  62.1 2.6 %copy-start.10 = (f32[64,256]{1,0:T(8,128)S(1)}, f32[64,256]{1,0:T(8,128)}, u32[]{:S(2)}) copy-start(f32[64,256]{1,0:T(8,128)} %param.15) | copy-start | bytes 196612
  62.1 3.4 %copy-start.8 = (f32[256,128]{1,0:T(8,128)S(1)}, f32[256,128]{1,0:T(8,128)}, u32[]{:S(2)}) copy-start(f32[256,128]{1,0:T(8,128)} %param.17) | copy-start | bytes 393220
  62.1 3.4 %copy-start.12 = (f32[64,128]{1,0:T(8,128)S(1)}, f32[64,128]{1,0:T(8,128)}, u32[]{:S(2)}) copy-start(f32[64,128]{1,0:T(8,128)} %param.16) | copy-start | bytes 98308
  62.1 5.9 %copy-start.7 = (f32[256,256]{1,0:T(8,128)S(1)}, f32[256,256]{1,0:T(8,128)}, u32[]{:S(2)}) copy-start(f32[256,256]{1,0:T(8,128)} %param.14) | copy-start | bytes 786436
  64.7 5.7 %copy-start.5 = (f32[5,256,128]{2,1,0:T(8,128)S(1)}, f32[5,256,128]{2,1,0:T(8,128)}, u32[]{:S(2)}) copy-start(f32[5,256,128]{2,1,0:T(8,128)} %param.19) | copy-start | bytes 1966084
  64.7 7.8 %copy-start.6 = (f32[5,128,128]{2,1,0:T(8,128)S(1)}, f32[5,128,128]{2,1,0:T(8,128)}, u32[]{:S(2)}) copy-start(f32[5,128,128]{2,1,0:T(8,128)} %param.18) | copy-start | bytes 983044
  65.9 59.7 %copy-start.9 = (f32[256,128]{1,0:T(8,128)S(1)}, f32[256,128]{1,0:T(8,128)}, u32[]{:S(2)}) copy-start(f32[256,128]{1,0:T(8,128)} %param.23) | copy-start | bytes 393220
  65.9 59.8 %copy-start.13 = (f32[64,128]{1,0:T(8,128)S(1)}, f32[64,128]{1,0:T(8,128)}, u32[]{:S(2)}) copy-start(f32[64,128]{1,0:T(8,128)} %param.22) | copy-start | bytes 98308
  65.9 4.5 %collective-permute-start.4 = (f32[4,128]{1,0:T(4,128)S(1)}, f32[4,128]{1,0:T(4,128)S(1)}, u32[]{:S(2)}, u32[]{:S(2)}) collective-permute-start(f32[4,128]{1,0:T(4,128)S(1)} %fusion.6), channel_id=1, source_target_pairs={{0,1},{1,0},{2,3},{3,2},{4,5},{5,4},{6,7},{7,6},{8,9},{9,8},{10,11... | collective-permute-start | bytes 6152 | tf_op jit(solution)/shard_map/ppermute | solution.py:34
  69.1 57.0 %copy-start.11 = (f32[256,64]{0,1:T(8,128)S(1)}, f32[256,64]{0,1:T(8,128)}, u32[]{:S(2)}) copy-start(f32[256,64]{0,1:T(8,128)} %param.24) | copy-start | bytes 196612
  70.6 5.2 %collective-permute-start.5 = (f32[4,128]{1,0:T(4,128)S(1)}, f32[4,128]{1,0:T(4,128)S(1)}, u32[]{:S(2)}, u32[]{:S(2)}) collective-permute-start(f32[4,128]{1,0:T(4,128)S(1)} %fusion.33), channel_id=1, source_target_pairs={{0,2},{2,0},{1,3},{3,1},{4,6},{6,4},{5,7},{7,5},{8,10},{10,8},{9,1... | collective-permute-start | bytes 6152 | tf_op jit(solution)/shard_map/ppermute | solution.py:34
  76.0 8.2 %collective-permute-start.6 = (f32[4,128]{1,0:T(4,128)S(1)}, f32[4,128]{1,0:T(4,128)S(1)}, u32[]{:S(2)}, u32[]{:S(2)}) collective-permute-start(f32[4,128]{1,0:T(4,128)S(1)} %fusion.31), channel_id=1, source_target_pairs={{0,4},{4,0},{1,5},{5,1},{2,6},{6,2},{3,7},{7,3},{8,12},{12,8},{9,1... | collective-permute-start | bytes 6152 | tf_op jit(solution)/shard_map/ppermute | solution.py:34
  84.4 4.3 %collective-permute-start.7 = (f32[4,128]{1,0:T(4,128)S(1)}, f32[4,128]{1,0:T(4,128)S(1)}, u32[]{:S(2)}, u32[]{:S(2)}) collective-permute-start(f32[4,128]{1,0:T(4,128)S(1)} %fusion.29), channel_id=1, source_target_pairs={{0,8},{8,0},{1,9},{9,1},{2,10},{10,2},{3,11},{11,3},{4,12},{12,4},... | collective-permute-start | bytes 6152 | tf_op jit(solution)/shard_map/ppermute | solution.py:34
  88.9 5.8 %collective-permute-start.8 = (f32[4,128]{1,0:T(4,128)S(1)}, f32[4,128]{1,0:T(4,128)S(1)}, u32[]{:S(2)}, u32[]{:S(2)}) collective-permute-start(f32[4,128]{1,0:T(4,128)S(1)} %fusion.27), channel_id=1, source_target_pairs={{0,16},{16,0},{1,17},{17,1},{2,18},{18,2},{3,19},{19,3},{4,20},{20... | collective-permute-start | bytes 6152 | tf_op jit(solution)/shard_map/ppermute | solution.py:34
  (1 other events, 0.7 us)
where the time goes:
time: 128 us
  local copies, waits for them, and re-layouts  33.6 us (26%)
  starting transfers between devices  29.6 us (23%)
  blocking collectives  28.3 us (22%)
  waiting for transfers between devices  13.9 us (11%)
  matrix products  13.4 us (10%)
  other arithmetic  8.61 us (7%)
    all_gather x1, blocking collectives, local(): shard_piece = lax.all_gather(skeleton[None], 'row', axis=0, tiled=True)  28.3 us
    ppermute x5, starting transfers between devices, partner_2(): return lax.ppermute(block, axis, route)  13.5 us
    ppermute x5, waiting for transfers between devices, partner_2(): return lax.ppermute(block, axis, route)  12.8 us
    ppermute x2, starting transfers between devices, extended(): after = lax.ppermute(first, axis, down)  9.4 us
    ppermute x2, starting transfers between devices, extended(): before = lax.ppermute(last, axis, up)  6.69 us
    slice x2, local copies, waits for them, and re-layouts, extended(): last = lax.slice_in_dim(x, length - width, length, axis=dim)  6.02 us
    slice x2, local copies, waits for them, and re-layouts, extended(): first = lax.slice_in_dim(x, 0, width, axis=dim)  4.95 us
    ppermute x1, local copies, waits for them, and re-layouts, extended(): before = lax.ppermute(last, axis, up)  4.6 us
  transfers between devices with their start and end apart: 9, of which 7 were waited for; matrix products, arithmetic and copies ran while one was open for 9% of the time, Pallas kernels for 0%

commit v1 on v0

--- a/solution.py
+++ b/solution.py
@@ -116,7 +116,9 @@
         )
         joined = jnp.concatenate([left_half, right_half], axis=-1)
         skeleton = jnp.dot(joined, merge_parent[merge_level], precision=full_precision)
-    shard_piece = lax.all_gather(skeleton[None], "row", axis=0, tiled=True)
+    shard_piece = jnp.concatenate(
+        jax.lax.all_to_all(jnp.stack([skeleton[None]] * jax.lax.axis_size("row")), "row", 0, 0), 0
+    )
     piece_rows = shard_piece.shape[0]
     top_rows = top_inverse
     top_rows = top_rows.reshape(piece_rows, SKEL, SKEL)

time: 128 us -> 127 us (level)
  blocking collectives: 28.3 us -> 0 us
  starting transfers between devices: 29.6 us -> 46.6 us
  matrix products: 13.4 us -> 18.5 us
  waiting for transfers between devices: 13.9 us -> 18.9 us
    all_gather x1 -> x0, blocking collectives: 28.3 us -> none  [local(): shard_piece = lax.all_gather(skeleton[None], 'row', axis=0, tiled=True)]
    all_to_all x0 -> x1, starting transfers between devices: none -> 16.7 us  [local(): jax.lax.all_to_all(jnp.stack([skeleton[None]] * jax.lax.axis_size('row'))...]
    all_to_all x0 -> x1, waiting for transfers between devices: none -> 6.4 us  [local(): jax.lax.all_to_all(jnp.stack([skeleton[None]] * jax.lax.axis_size('row'))...]
    dot_general x5, matrix products: 0.84 us -> 2.52 us  [local(): jnp.dot(boundary, child_map[:, :SKEL], precision=full_precision)]
    dot_general x5, matrix products: 0.87 us -> 2.54 us  [local(): jnp.dot(boundary, child_map[:, SKEL:], precision=full_precision)]
    ppermute x5, waiting for transfers between devices: 12.8 us -> 11.4 us  [partner_2(): return lax.ppermute(block, axis, route)]
    unnamed x34 -> x32, local copies, waits for them, and re-layouts: 3.93 us -> 3.94 us
  transfers between devices with their start and end apart: 9 -> 10, of which waited for: 7 -> 8; matrix products, arithmetic and copies ran while one was open for 9% -> 11% of each run, Pallas kernels for 0% -> 0%
where the time goes in v1:
time: 127 us; the launch traced here: 126 us
  starting transfers between devices  46.6 us (37%)
  local copies, waits for them, and re-layouts  32.8 us (26%)
  waiting for transfers between devices  18.9 us (15%)
  matrix products  18.5 us (15%)
  other arithmetic  8.61 us (7%)
    all_to_all x1, starting transfers between devices, local(): jax.lax.all_to_all(jnp.stack([skeleton[None]] * jax.lax.axis_size('row'))...  16.7 us
    ppermute x5, starting transfers between devices, partner_2(): return lax.ppermute(block, axis, route)  13.8 us
    ppermute x5, waiting for transfers between devices, partner_2(): return lax.ppermute(block, axis, route)  11.4 us
    ppermute x2, starting transfers between devices, extended(): after = lax.ppermute(first, axis, down)  9.4 us
    ppermute x2, starting transfers between devices, extended(): before = lax.ppermute(last, axis, up)  6.68 us
    all_to_all x1, waiting for transfers between devices, local(): jax.lax.all_to_all(jnp.stack([skeleton[None]] * jax.lax.axis_size('row'))...  6.4 us
    slice x2, local copies, waits for them, and re-layouts, extended(): last = lax.slice_in_dim(x, length - width, length, axis=dim)  6.04 us
    slice x2, local copies, waits for them, and re-layouts, extended(): first = lax.slice_in_dim(x, 0, width, axis=dim)  4.34 us
  transfers between devices with their start and end apart: 10, of which 8 were waited for; matrix products, arithmetic and copies ran while one was open for 11% of the time, Pallas kernels for 0%

profile of v1, /device:TPU:1, one launch (start us, length us, event | category | flops | bytes accessed | tf_op | source)
XLA Modules:
  0.0 125.8 jit_solution(4987139288974259671)
XLA Ops:
  0.0 2.1 %reshape.43 = bf16[4,16,16,4,64]{4,3,2,1,0:T(4,128)(2,1)S(1)} reshape(bf16[4,16,16,1,1,256]{5,2,4,3,1,0:T(8,128)(2,1)} %param.13) | data formatting | bytes 1048576 | tf_op jit(solution)/shard_map/reshape | solution.py:91
  3.1 3.5 %collective-permute-start = (bf16[4,16,16,1,64]{4,1,3,2,0:T(8,128)(2,1)S(1)}, bf16[4,16,16,1,64]{4,1,3,2,0:T(8,128)(2,1)S(1)}, u32[]{:S(2)}, u32[]{:S(2)}) collective-permute-start(bf16[4,16,16,1,64]{4,1,3,2,0:T(8,128)(2,1)S(1)} %copy.84), channel_id=1, source_target_pairs={{0,32},{32,64},{64,96},{96,128},{128,160},{160,192},{192,224},{224... | collective-permute-start | bytes 393224 | tf_op jit(solution)/shard_map/ppermute | solution.py:21
  6.7 3.4 %collective-permute-start.1 = (bf16[4,16,16,1,64]{4,1,3,2,0:T(8,128)(2,1)S(1)}, bf16[4,16,16,1,64]{4,1,3,2,0:T(8,128)(2,1)S(1)}, u32[]{:S(2)}, u32[]{:S(2)}) collective-permute-start(bf16[4,16,16,1,64]{4,1,3,2,0:T(8,128)(2,1)S(1)} %copy.85), channel_id=1, source_target_pairs={{32,0},{64,32},{96,64},{128,96},{160,128},{192,160},{224,192},{256... | collective-permute-start | bytes 393224 | tf_op jit(solution)/shard_map/ppermute | solution.py:22
  12.6 2.4 %fusion.101 = (bf16[4,16,16,6,1]{4,1,3,2,0:T(8,128)(2,1)}, bf16[4,16,16,6,1]{4,1,3,2,0:T(8,128)(2,1)}) fusion(bf16[4,16,16,6,64]{4,1,3,2,0:T(8,128)(2,1)S(1)} %constant_dynamic-update-slice_fusion), kind=kLoop, calls=%fused_computation.151 | loop fusion | bytes 49152 | tf_op jit(solution)/shard_map/slice | solution.py:19
  15.0 3.7 %copy.58 = bf16[4,16,16,6,1]{2,1,4,3,0:T(8,128)(2,1)S(1)} copy(bf16[4,16,16,6,1]{4,1,3,2,0:T(8,128)(2,1)} %get-tuple-element.19) | data formatting | bytes 24576 | tf_op jit(solution)/shard_map/slice | solution.py:19
  18.6 3.2 %collective-permute-start.2 = (bf16[4,16,16,6,1]{2,1,4,3,0:T(8,128)(2,1)S(1)}, bf16[4,16,16,6,1]{2,1,4,3,0:T(8,128)(2,1)S(1)}, u32[]{:S(2)}, u32[]{:S(2)}) collective-permute-start(bf16[4,16,16,6,1]{2,1,4,3,0:T(8,128)(2,1)S(1)} %copy.58), channel_id=1, source_target_pairs={{0,1},{1,2},{2,3},{3,4},{4,5},{5,6},{6,7},{7,8},{8,9},{9,10},{10,1... | collective-permute-start | bytes 36872 | tf_op jit(solution)/shard_map/ppermute | solution.py:21
  21.8 3.6 %copy.59 = bf16[4,16,16,6,1]{2,1,4,3,0:T(8,128)(2,1)S(1)} copy(bf16[4,16,16,6,1]{4,1,3,2,0:T(8,128)(2,1)} %get-tuple-element.20) | data formatting | bytes 24576 | tf_op jit(solution)/shard_map/slice | solution.py:20
  25.4 6.0 %collective-permute-start.3 = (bf16[4,16,16,6,1]{2,1,4,3,0:T(8,128)(2,1)S(1)}, bf16[4,16,16,6,1]{2,1,4,3,0:T(8,128)(2,1)S(1)}, u32[]{:S(2)}, u32[]{:S(2)}) collective-permute-start(bf16[4,16,16,6,1]{2,1,4,3,0:T(8,128)(2,1)S(1)} %copy.59), channel_id=1, source_target_pairs={{1,0},{2,1},{3,2},{4,3},{5,4},{6,5},{7,6},{8,7},{9,8},{10,9},{11,1... | collective-permute-start | bytes 36872 | tf_op jit(solution)/shard_map/ppermute | solution.py:22
  32.2 3.8 %copy.60 = bf16[4,16,16,6,1]{4,1,3,2,0:T(8,128)(2,1)} copy(bf16[4,16,16,6,1]{2,1,4,3,0:T(8,128)(2,1)S(1)} %collective-permute-done.2) | data formatting | bytes 24576 | tf_op jit(solution)/shard_map/ppermute | solution.py:21
  36.0 3.8 %copy.61 = bf16[4,16,16,6,1]{4,1,3,2,0:T(8,128)(2,1)} copy(bf16[4,16,16,6,1]{2,1,4,3,0:T(8,128)(2,1)S(1)} %collective-permute-done.3) | data formatting | bytes 24576 | tf_op jit(solution)/shard_map/ppermute | solution.py:22
  39.9 3.8 %fusion.98 = (f32[4,16,16,6,66]{4,1,3,2,0:T(8,128)S(1)}, bf16[4,16,16,6,66]{4,1,3,2,0:T(8,128)(2,1)S(1)}) fusion(bf16[4,16,16,6,1]{4,1,3,2,0:T(8,128)(2,1)} %copy.61, bf16[4,16,16,6,64]{4,1,3,2,0:T(8,128)(2,1)} %copy-done.2, bf16[4,16,16,6,1]{4,1,3,2,0:T(8,128)(2,1)} %copy.60), kind=kLoop, calls=%fused_computation.148 | loop fusion | flops 2838528 | bytes 3244032 | tf_op jit(solution)/shard_map/convert_element_type | solution.py:93
  45.9 3.5 %fusion.1 = f32[4,16,16,6,66]{4,1,3,2,0:T(8,128)S(1)} fusion(f32[4,16,6,66,16]{3,4,2,1,0:T(8,128)S(1)} %fusion.3, bf16[4,16,16,6,66]{4,1,3,2,0:T(8,128)(2,1)S(1)} %get-tuple-element.6, f32[16,16,1,1,1]{1,0,4,3,2:T(8,128)S(1)} %copy-done.13, f32[16,16,6,66]{3,0,2,1:T(8,128)S(1)} %get-tuple-element.18, f32[16,16,6,66]{3,0,2,1:T(8,128)S(1)} %get-tuple-element.17), kind=kOutput, calls=%fused_computation.3 | convolution fusion | flops 79478784 | bytes 4867072 | tf_op jit(solution)/shard_map/ik,fkjrc->fijrc/dot_general | solution.py:51
  58.2 2.4 %copy.72 = f32[4,16,16,4,64]{4,3,2,1,0:T(4,128)} copy(f32[4,16,16,4,64]{4,1,3,2,0:T(8,128)S(1)} %fusion.2) | data formatting | bytes 2097152 | tf_op jit(solution)/shard_map/sub | solution.py:100
  60.6 2.5 %reshape.44 = f32[4,256,256]{2,1,0:T(8,128)S(1)} reshape(f32[4,16,16,4,64]{4,3,2,1,0:T(4,128)} %copy.72) | data formatting | bytes 2097152 | tf_op jit(solution)/shard_map/reshape | solution.py:100
  66.2 2.0 %fusion.12 = f32[4,256,256]{1,2,0:T(8,128)S(1)} fusion(f32[4,256,256]{2,1,0:T(8,128)S(1)} %reshape.44, f32[256,256]{1,0:T(8,128)} %param.14), kind=kOutput, calls=%fused_computation.34 | convolution fusion | flops 805306368 | bytes 2359296 | tf_op jit(solution)/shard_map/nm,fml->fnl/dot_general | solution.py:101
  68.8 2.4 %collective-permute-start.5 = (f32[4,128]{1,0:T(4,128)S(1)}, f32[4,128]{1,0:T(4,128)S(1)}, u32[]{:S(2)}, u32[]{:S(2)}) collective-permute-start(f32[4,128]{1,0:T(4,128)S(1)} %fusion.34), channel_id=1, source_target_pairs={{0,2},{2,0},{1,3},{3,1},{4,6},{6,4},{5,7},{7,5},{8,10},{10,8},{9,1... | collective-permute-start | bytes 6152 | tf_op jit(solution)/shard_map/ppermute | solution.py:34
  71.4 2.7 %collective-permute-done.5 = f32[4,128]{1,0:T(4,128)S(1)} collective-permute-done((f32[4,128]{1,0:T(4,128)S(1)}, f32[4,128]{1,0:T(4,128)S(1)}, u32[]{:S(2)}, u32[]{:S(2)}) %collective-permute-start.5) | collective-permute-done | bytes 2080 | tf_op jit(solution)/shard_map/ppermute | solution.py:34
  74.2 4.7 %collective-permute-start.6 = (f32[4,128]{1,0:T(4,128)S(1)}, f32[4,128]{1,0:T(4,128)S(1)}, u32[]{:S(2)}, u32[]{:S(2)}) collective-permute-start(f32[4,128]{1,0:T(4,128)S(1)} %fusion.32), channel_id=1, source_target_pairs={{0,4},{4,0},{1,5},{5,1},{2,6},{6,2},{3,7},{7,3},{8,12},{12,8},{9,1... | collective-permute-start | bytes 6152 | tf_op jit(solution)/shard_map/ppermute | solution.py:34
  79.1 3.3 %collective-permute-done.6 = f32[4,128]{1,0:T(4,128)S(1)} collective-permute-done((f32[4,128]{1,0:T(4,128)S(1)}, f32[4,128]{1,0:T(4,128)S(1)}, u32[]{:S(2)}, u32[]{:S(2)}) %collective-permute-start.6) | collective-permute-done | bytes 2080 | tf_op jit(solution)/shard_map/ppermute | solution.py:34
  84.7 2.2 %collective-permute-done.7 = f32[4,128]{1,0:T(4,128)S(1)} collective-permute-done((f32[4,128]{1,0:T(4,128)S(1)}, f32[4,128]{1,0:T(4,128)S(1)}, u32[]{:S(2)}, u32[]{:S(2)}) %collective-permute-start.7) | collective-permute-done | bytes 2080 | tf_op jit(solution)/shard_map/ppermute | solution.py:34
  87.2 2.8 %collective-permute-start.8 = (f32[4,128]{1,0:T(4,128)S(1)}, f32[4,128]{1,0:T(4,128)S(1)}, u32[]{:S(2)}, u32[]{:S(2)}) collective-permute-start(f32[4,128]{1,0:T(4,128)S(1)} %fusion.28), channel_id=1, source_target_pairs={{0,16},{16,0},{1,17},{17,1},{2,18},{18,2},{3,19},{19,3},{4,20},{20... | collective-permute-start | bytes 6152 | tf_op jit(solution)/shard_map/ppermute | solution.py:34
  90.1 2.8 %collective-permute-done.8 = f32[4,128]{1,0:T(4,128)S(1)} collective-permute-done((f32[4,128]{1,0:T(4,128)S(1)}, f32[4,128]{1,0:T(4,128)S(1)}, u32[]{:S(2)}, u32[]{:S(2)}) %collective-permute-start.8) | collective-permute-done | bytes 2080 | tf_op jit(solution)/shard_map/ppermute | solution.py:34
  93.8 16.7 %all-to-all-start = ((f32[16,1,4,128]{3,2,1,0:T(4,128)}), f32[16,1,4,128]{3,2,1,0:T(4,128)S(1)}, u32[]{:S(2)}, u32[]{:S(2)}) async-start(f32[16,1,4,128]{3,2,1,0:T(4,128)} %stack.3), calls=%async_computation | async-start | bytes 65536 | tf_op jit(solution)/shard_map/all_to_all | solution.py:120
  111.5 6.4 %all-to-all-done = f32[16,1,4,128]{3,2,1,0:T(4,128)S(1)} async-done(((f32[16,1,4,128]{3,2,1,0:T(4,128)}), f32[16,1,4,128]{3,2,1,0:T(4,128)S(1)}, u32[]{:S(2)}, u32[]{:S(2)}) %all-to-all-start) | async-done | bytes 32800 | tf_op jit(solution)/shard_map/all_to_all | solution.py:120
  (93 shorter events, 31.6 us)
Async XLA Ops:
  0.0 117.9 %copy-start = (f32[2048,128]{1,0:T(8,128)S(1)}, f32[2048,128]{1,0:T(8,128)}, u32[]{:S(2)}) copy-start(f32[2048,128]{1,0:T(8,128)} %param.21) | copy-start | bytes 3145732
  3.1 7.9 %collective-permute-start = (bf16[4,16,16,1,64]{4,1,3,2,0:T(8,128)(2,1)S(1)}, bf16[4,16,16,1,64]{4,1,3,2,0:T(8,128)(2,1)S(1)}, u32[]{:S(2)}, u32[]{:S(2)}) collective-permute-start(bf16[4,16,16,1,64]{4,1,3,2,0:T(8,128)(2,1)S(1)} %copy.84), channel_id=1, source_target_pairs={{0,32},{32,64},{64,96},{96,128},{128,160},{160,192},{192,224},{224... | collective-permute-start | bytes 393224 | tf_op jit(solution)/shard_map/ppermute | solution.py:21
  6.7 5.8 %collective-permute-start.1 = (bf16[4,16,16,1,64]{4,1,3,2,0:T(8,128)(2,1)S(1)}, bf16[4,16,16,1,64]{4,1,3,2,0:T(8,128)(2,1)S(1)}, u32[]{:S(2)}, u32[]{:S(2)}) collective-permute-start(bf16[4,16,16,1,64]{4,1,3,2,0:T(8,128)(2,1)S(1)} %copy.85), channel_id=1, source_target_pairs={{32,0},{64,32},{96,64},{128,96},{160,128},{192,160},{224,192},{256... | collective-permute-start | bytes 393224 | tf_op jit(solution)/shard_map/ppermute | solution.py:22
  12.6 2.4 %copy-start.2 = (bf16[4,16,16,6,64]{4,1,3,2,0:T(8,128)(2,1)}, bf16[4,16,16,6,64]{4,1,3,2,0:T(8,128)(2,1)S(1)}, u32[]{:S(2)}) copy-start(bf16[4,16,16,6,64]{4,1,3,2,0:T(8,128)(2,1)S(1)} %constant_dynamic-update-slice_fusion) | copy-start | bytes 2359300
  15.0 16.5 %copy-start.4 = (f32[5,128,256]{2,1,0:T(8,128)S(1)}, f32[5,128,256]{2,1,0:T(8,128)}, u32[]{:S(2)}) copy-start(f32[5,128,256]{2,1,0:T(8,128)} %param.20) | copy-start | bytes 1966084
  18.6 13.6 %collective-permute-start.2 = (bf16[4,16,16,6,1]{2,1,4,3,0:T(8,128)(2,1)S(1)}, bf16[4,16,16,6,1]{2,1,4,3,0:T(8,128)(2,1)S(1)}, u32[]{:S(2)}, u32[]{:S(2)}) collective-permute-start(bf16[4,16,16,6,1]{2,1,4,3,0:T(8,128)(2,1)S(1)} %copy.58), channel_id=1, source_target_pairs={{0,1},{1,2},{2,3},{3,4},{4,5},{5,6},{6,7},{7,8},{8,9},{9,10},{10,1... | collective-permute-start | bytes 36872 | tf_op jit(solution)/shard_map/ppermute | solution.py:21
  25.4 10.6 %collective-permute-start.3 = (bf16[4,16,16,6,1]{2,1,4,3,0:T(8,128)(2,1)S(1)}, bf16[4,16,16,6,1]{2,1,4,3,0:T(8,128)(2,1)S(1)}, u32[]{:S(2)}, u32[]{:S(2)}) collective-permute-start(bf16[4,16,16,6,1]{2,1,4,3,0:T(8,128)(2,1)S(1)} %copy.59), channel_id=1, source_target_pairs={{1,0},{2,1},{3,2},{4,3},{5,4},{6,5},{7,6},{8,7},{9,8},{10,9},{11,1... | collective-permute-start | bytes 36872 | tf_op jit(solution)/shard_map/ppermute | solution.py:22
  50.2 1.6 %copy-start.1 = (f32[4,14,16,6,66]{4,1,3,2,0:T(8,128)}, f32[4,14,16,6,66]{4,1,3,2,0:T(8,128)S(1)}, u32[]{:S(2)}) copy-start(f32[4,14,16,6,66]{4,1,3,2,0:T(8,128)S(1)} %slice.198) | copy-start | bytes 4257796
  51.8 1.7 %copy-start.3 = (f32[4,16,16,6,66]{4,1,3,2,0:T(8,128)}, f32[4,16,16,6,66]{4,1,3,2,0:T(8,128)S(1)}, u32[]{:S(2)}) copy-start(f32[4,16,16,6,66]{4,1,3,2,0:T(8,128)S(1)} %pad_maximum_fusion) | copy-start | bytes 4866052
  54.5 2.1 %slice-start = ((f32[4,16,16,6,66]{4,1,3,2,0:T(8,128)}), f32[4,16,14,6,66]{4,1,3,2,0:T(8,128)S(1)}, s32[]{:S(2)}) async-start(f32[4,16,16,6,66]{4,1,3,2,0:T(8,128)} %copy-done.3), calls=%async_computation.1 | async-start | bytes 5505024 | tf_op jit(solution)/shard_map/slice | solution.py:70
  60.6 2.5 %copy-start.9 = (f32[64,256]{1,0:T(8,128)S(1)}, f32[64,256]{1,0:T(8,128)}, u32[]{:S(2)}) copy-start(f32[64,256]{1,0:T(8,128)} %param.15) | copy-start | bytes 196612
  60.6 3.4 %copy-start.7 = (f32[256,128]{1,0:T(8,128)S(1)}, f32[256,128]{1,0:T(8,128)}, u32[]{:S(2)}) copy-start(f32[256,128]{1,0:T(8,128)} %param.17) | copy-start | bytes 393220
  60.6 3.4 %copy-start.11 = (f32[64,128]{1,0:T(8,128)S(1)}, f32[64,128]{1,0:T(8,128)}, u32[]{:S(2)}) copy-start(f32[64,128]{1,0:T(8,128)} %param.16) | copy-start | bytes 98308
  63.1 5.6 %copy-start.5 = (f32[5,256,128]{2,1,0:T(8,128)S(1)}, f32[5,256,128]{2,1,0:T(8,128)}, u32[]{:S(2)}) copy-start(f32[5,256,128]{2,1,0:T(8,128)} %param.19) | copy-start | bytes 1966084
  63.1 8.1 %copy-start.6 = (f32[5,128,128]{2,1,0:T(8,128)S(1)}, f32[5,128,128]{2,1,0:T(8,128)}, u32[]{:S(2)}) copy-start(f32[5,128,128]{2,1,0:T(8,128)} %param.18) | copy-start | bytes 983044
  64.3 4.3 %collective-permute-start.4 = (f32[4,128]{1,0:T(4,128)S(1)}, f32[4,128]{1,0:T(4,128)S(1)}, u32[]{:S(2)}, u32[]{:S(2)}) collective-permute-start(f32[4,128]{1,0:T(4,128)S(1)} %fusion.6), channel_id=1, source_target_pairs={{0,1},{1,0},{2,3},{3,2},{4,5},{5,4},{6,7},{7,6},{8,9},{9,8},{10,11... | collective-permute-start | bytes 6152 | tf_op jit(solution)/shard_map/ppermute | solution.py:34
  68.3 55.3 %copy-start.8 = (f32[256,128]{1,0:T(8,128)S(1)}, f32[256,128]{1,0:T(8,128)}, u32[]{:S(2)}) copy-start(f32[256,128]{1,0:T(8,128)} %param.23) | copy-start | bytes 393220
  68.3 55.3 %copy-start.12 = (f32[64,128]{1,0:T(8,128)S(1)}, f32[64,128]{1,0:T(8,128)}, u32[]{:S(2)}) copy-start(f32[64,128]{1,0:T(8,128)} %param.22) | copy-start | bytes 98308
  68.3 55.7 %copy-start.10 = (f32[256,64]{0,1:T(8,128)S(1)}, f32[256,64]{0,1:T(8,128)}, u32[]{:S(2)}) copy-start(f32[256,64]{0,1:T(8,128)} %param.24) | copy-start | bytes 196612
  68.8 5.2 %collective-permute-start.5 = (f32[4,128]{1,0:T(4,128)S(1)}, f32[4,128]{1,0:T(4,128)S(1)}, u32[]{:S(2)}, u32[]{:S(2)}) collective-permute-start(f32[4,128]{1,0:T(4,128)S(1)} %fusion.34), channel_id=1, source_target_pairs={{0,2},{2,0},{1,3},{3,1},{4,6},{6,4},{5,7},{7,5},{8,10},{10,8},{9,1... | collective-permute-start | bytes 6152 | tf_op jit(solution)/shard_map/ppermute | solution.py:34
  74.2 8.2 %collective-permute-start.6 = (f32[4,128]{1,0:T(4,128)S(1)}, f32[4,128]{1,0:T(4,128)S(1)}, u32[]{:S(2)}, u32[]{:S(2)}) collective-permute-start(f32[4,128]{1,0:T(4,128)S(1)} %fusion.32), channel_id=1, source_target_pairs={{0,4},{4,0},{1,5},{5,1},{2,6},{6,2},{3,7},{7,3},{8,12},{12,8},{9,1... | collective-permute-start | bytes 6152 | tf_op jit(solution)/shard_map/ppermute | solution.py:34
  82.6 4.3 %collective-permute-start.7 = (f32[4,128]{1,0:T(4,128)S(1)}, f32[4,128]{1,0:T(4,128)S(1)}, u32[]{:S(2)}, u32[]{:S(2)}) collective-permute-start(f32[4,128]{1,0:T(4,128)S(1)} %fusion.30), channel_id=1, source_target_pairs={{0,8},{8,0},{1,9},{9,1},{2,10},{10,2},{3,11},{11,3},{4,12},{12,4},... | collective-permute-start | bytes 6152 | tf_op jit(solution)/shard_map/ppermute | solution.py:34
  87.2 5.8 %collective-permute-start.8 = (f32[4,128]{1,0:T(4,128)S(1)}, f32[4,128]{1,0:T(4,128)S(1)}, u32[]{:S(2)}, u32[]{:S(2)}) collective-permute-start(f32[4,128]{1,0:T(4,128)S(1)} %fusion.28), channel_id=1, source_target_pairs={{0,16},{16,0},{1,17},{17,1},{2,18},{18,2},{3,19},{19,3},{4,20},{20... | collective-permute-start | bytes 6152 | tf_op jit(solution)/shard_map/ppermute | solution.py:34
  93.8 24.1 %all-to-all-start = ((f32[16,1,4,128]{3,2,1,0:T(4,128)}), f32[16,1,4,128]{3,2,1,0:T(4,128)S(1)}, u32[]{:S(2)}, u32[]{:S(2)}) async-start(f32[16,1,4,128]{3,2,1,0:T(4,128)} %stack.3), calls=%async_computation | async-start | bytes 65536 | tf_op jit(solution)/shard_map/all_to_all | solution.py:120
  (1 other events, 0.7 us)
